TPU v7x, 32 devices: a whole 2x2x4 slice. The times are simulated.
32 devices in a mesh: path: 16 (over z, x, core), row: 2 (over y).
Axes of the slice: x: 2, y: 2, z: 4, core: 2. Of those that a mesh axis runs over, the one named last changes fastest.
Arguments:
- main_field: bfloat16 [2, 36, 512, 512], P(None, None, 'path', 'row'), may hold values from -6 to 6
- reflect: float32 [9], replicated, may hold values from 0.5 to 1
- curvature: float32 [9], replicated, may hold values from 100 to 1000
- position: float32 [9], replicated, may hold values from 0 to 1
- wave: float32 [4], replicated, may hold values from 0.8 to 1.6
- ghost_pair: int32 [16, 2], replicated, may hold values from 0 to 8, as said below
- ghost_case: int32 [16], replicated, may hold values from 0 to 3, as said below
Outputs:
- glare: float32 [4, 512, 512], P(None, 'path', 'row')
Inputs may be any that keep to these rules, and one draw needn't show every extreme that they name: `ghost_pair`: column 0 is the start surface a and column 1 the turning surface b of a ghost path, with b < a; the triples (a, b, ghost_case) of all ghost paths are distinct. `ghost_case`: together with ghost_pair, no triple (start surface, turning surface, case) appears twice.
All inputs are finite; a program needn't handle non-finite values.
Results may differ from a plain program's by a relative error of at most 0.0003.
Values may be sent and summed in bfloat16 or wider, within the bound.
A program may use at most 128 MiB of HBM per device.

v0:
```python
import math

import jax
import jax.numpy as jnp
from jax import lax
from jax.sharding import PartitionSpec as P

NG = 512
CASES = 4
SURF = 9
GH_DEV = 1


spread_scale = 2000.0


def tables(grid_cells):
    counter = jnp.arange(grid_cells, dtype=jnp.int32)
    angles = (
        2.0
        * math.pi
        / grid_cells
        * (counter[:, None] * counter[None, :] % grid_cells).astype(jnp.float32)
    )
    return (jnp.cos(angles), jnp.sin(angles))


def complex_apply(contract, real_part, imag_part, cosine_table, sine_table, inverse):
    if inverse:
        new_real = (contract(real_part, cosine_table) - contract(imag_part, sine_table)) / float(NG)
        new_imag = (contract(imag_part, cosine_table) + contract(real_part, sine_table)) / float(NG)
    else:
        new_real = contract(real_part, cosine_table) + contract(imag_part, sine_table)
        new_imag = contract(imag_part, cosine_table) - contract(real_part, sine_table)
    return (new_real, new_imag)


def along_last(values, table):
    return jnp.einsum("grv,vk->grk", values, table, precision=lax.Precision.HIGHEST)


def along_rows(values, table):
    return jnp.einsum("ur,grc->guc", table, values, precision=lax.Precision.HIGHEST)


def local(main_field, reflect, curvature, position, wave, ghost_pair, ghost_case):
    path_count = lax.axis_size("path")
    row_count = lax.axis_size("row")
    slab_cells = NG // row_count
    piece_rows = NG // path_count
    ghosts = GH_DEV * path_count
    own_slots = lax.axis_index("path") * GH_DEV + jnp.arange(GH_DEV, dtype=jnp.int32)
    field_ids = ghost_case * SURF + ghost_pair[:, 0]
    own_pair = ghost_pair[own_slots]
    own_case = ghost_case[own_slots]
    picked = main_field[:, field_ids]
    picked = picked.reshape(2, path_count, GH_DEV, piece_rows, slab_cells)
    arrived = lax.all_to_all(picked, "path", split_axis=1, concat_axis=3, tiled=True)
    start_field = arrived.reshape(2, GH_DEV, NG, slab_cells)
    surfaces = jnp.arange(SURF, dtype=jnp.int32)
    case_range = jnp.arange(CASES, dtype=jnp.int32)
    start_hot = (own_pair[:, 0:1] == surfaces[None, :]).astype(jnp.float32)
    turn_hot = (own_pair[:, 1:2] == surfaces[None, :]).astype(jnp.float32)
    case_hot = (own_case[:, None] == case_range[None, :]).astype(jnp.float32)
    start_gain = jnp.sum(start_hot * reflect[None, :], 1)
    turn_gain = jnp.sum(turn_hot * reflect[None, :], 1)
    screen_power = jnp.sum(turn_hot * curvature[None, :], 1)
    distance = jnp.sum(start_hot * position[None, :], 1) - jnp.sum(turn_hot * position[None, :], 1)
    wavelength = jnp.sum(case_hot * wave[None, :], 1)
    coefficient = spread_scale * wavelength * distance
    slab_offset = lax.axis_index("row") * slab_cells
    all_index = jnp.arange(NG, dtype=jnp.int32)
    slab_index = jnp.arange(slab_cells, dtype=jnp.int32) + slab_offset
    full_shift = ((all_index + NG // 2) % NG - NG // 2).astype(jnp.float32)
    slab_shift = ((slab_index + NG // 2) % NG - NG // 2).astype(jnp.float32)
    frequency = (
        slab_shift[:, None] * slab_shift[:, None] + full_shift[None, :] * full_shift[None, :]
    ) / float(NG * NG)
    phase = coefficient[:, None, None] * frequency[None]
    transfer_cos = jnp.cos(phase)
    transfer_sin = -jnp.sin(phase)
    slab_centred = (slab_index - NG // 2).astype(jnp.float32) / float(NG)
    full_centred = (all_index - NG // 2).astype(jnp.float32) / float(NG)
    radial = (
        full_centred[:, None] * full_centred[:, None]
        + slab_centred[None, :] * slab_centred[None, :]
    )
    screen = screen_power[:, None, None] * radial[None]
    screen_cos = turn_gain[:, None, None] * jnp.cos(screen)
    screen_sin = turn_gain[:, None, None] * jnp.sin(screen)
    cosine_table, sine_table = tables(NG)

    def propagate(real_part, imag_part):
        real_part, imag_part = complex_apply(
            along_rows, real_part, imag_part, cosine_table, sine_table, False
        )
        real_part, imag_part = (
            lax.all_to_all(real_part, "row", split_axis=1, concat_axis=2, tiled=True),
            lax.all_to_all(imag_part, "row", split_axis=1, concat_axis=2, tiled=True),
        )
        real_part, imag_part = complex_apply(
            along_last, real_part, imag_part, cosine_table, sine_table, False
        )
        real_part, imag_part = (
            real_part * transfer_cos - imag_part * transfer_sin,
            real_part * transfer_sin + imag_part * transfer_cos,
        )
        real_part, imag_part = complex_apply(
            along_last, real_part, imag_part, cosine_table, sine_table, True
        )
        real_part, imag_part = (
            lax.all_to_all(real_part, "row", split_axis=2, concat_axis=1, tiled=True),
            lax.all_to_all(imag_part, "row", split_axis=2, concat_axis=1, tiled=True),
        )
        return complex_apply(along_rows, real_part, imag_part, cosine_table, sine_table, True)

    real_part = start_gain[:, None, None] * start_field[0].astype(jnp.float32)
    imag_part = start_gain[:, None, None] * start_field[1].astype(jnp.float32)
    real_part, imag_part = propagate(real_part, imag_part)
    real_part, imag_part = (
        screen_cos * real_part - screen_sin * imag_part,
        screen_sin * real_part + screen_cos * imag_part,
    )
    real_part, imag_part = propagate(real_part, imag_part)
    intensity = real_part * real_part + imag_part * imag_part
    case_terms = jnp.sum(case_hot[:, :, None, None] * intensity[:, None], 0)
    glare_image = lax.psum_scatter(case_terms, "path", scatter_dimension=1, tiled=True)
    return glare_image * (CASES / ghosts)


def solution(mesh):
    in_specs = (P(None, None, "path", "row"), P(), P(), P(), P(), P(), P())
    out_specs = P(None, "path", "row")
    return jax.shard_map(local, mesh=mesh, in_specs=in_specs, out_specs=out_specs, check_vma=False)
```

profile of v0, /device:TPU:0, one launch (start us, length us, event | category | flops | bytes accessed | tf_op | source)
XLA Modules:
  0.0 369.1 jit_solution(7611206632329737712)
XLA Ops:
  9.2 7.4 %all-to-all-start = ((bf16[2,16,1,32,256]{4,3,0,2,1:T(8,128)(2,1)}), bf16[2,16,1,32,256]{4,3,0,2,1:T(8,128)(2,1)S(1)}, u32[]{:S(2)}, u32[]{:S(2)}) async-start(bf16[2,16,1,32,256]{4,3,0,2,1:T(8,128)(2,1)} %bitcast.7), calls=%async_computation | async-start | bytes 1048576 | tf_op jit(solution)/shard_map/all_to_all | solution.py:58
  21.9 9.0 %all-to-all-done = bf16[2,16,1,32,256]{4,3,0,2,1:T(8,128)(2,1)S(1)} async-done(((bf16[2,16,1,32,256]{4,3,0,2,1:T(8,128)(2,1)}), bf16[2,16,1,32,256]{4,3,0,2,1:T(8,128)(2,1)S(1)}, u32[]{:S(2)}, u32[]{:S(2)}) %all-to-all-start) | async-done | bytes 524320 | tf_op jit(solution)/shard_map/all_to_all | solution.py:58
  73.1 6.2 %fusion.63 = f32[256,512]{1,0:T(8,128)S(1)} fusion(f32[256,512]{0,1:T(8,128)S(1)} %bitcast.134), kind=kOutput, calls=%fused_computation.80 | convolution fusion | flops 808976384 | bytes 1048576 | tf_op jit(solution)/shard_map/grv,vk->grk/dot_general | solution.py:39
  85.2 5.9 %convolution_add_fusion.6 = f32[256,512]{1,0:T(8,128)S(1)} fusion(f32[256,512]{1,0:T(8,128)S(1)} %fusion.63, f32[256,512]{0,1:T(8,128)S(1)} %bitcast.131), kind=kOutput, calls=%fused_computation.19 | convolution fusion | flops 809107456 | bytes 1572864 | tf_op jit(solution)/shard_map/grv,vk->grk/dot_general | solution.py:39
  91.1 6.1 %convolution_subtract_fusion.6 = f32[256,512]{1,0:T(8,128)S(1)} fusion(f32[256,512]{1,0:T(8,128)S(1)} %fusion.59, f32[256,512]{0,1:T(8,128)S(1)} %bitcast.135), kind=kOutput, calls=%fused_computation.18 | convolution fusion | flops 809107456 | bytes 1572864 | tf_op jit(solution)/shard_map/grv,vk->grk/dot_general | solution.py:39
  97.2 6.9 %fusion.53 = f32[256,512]{1,0:T(8,128)S(1)} fusion(f32[256,512]{1,0:T(8,128)S(1)} %convolution_subtract_fusion.6, f32[256,512]{1,0:T(8,128)S(1)} %convolution_add_fusion.6, f32[]{:T(128)S(6)} %mul.531, f32[512]{0:T(512)S(1)} %fusion.86, f32[256]{0:T(256)S(1)} %get-tuple-element.36), kind=kOutput, calls=%fused_computation.75 | convolution fusion | flops 809762816 | bytes 1575940 | tf_op jit(solution)/shard_map/grv,vk->grk/dot_general | solution.py:39
  104.1 7.9 %fusion.57 = f32[256,512]{1,0:T(8,128)} fusion(f32[256,512]{1,0:T(8,128)S(1)} %convolution_subtract_fusion.6, f32[256,512]{1,0:T(8,128)S(1)} %convolution_add_fusion.6, f32[]{:T(128)S(6)} %mul.531, f32[512]{0:T(512)S(1)} %fusion.86, f32[256]{0:T(256)S(1)} %get-tuple-element.36), kind=kOutput, calls=%fused_computation.77 | convolution fusion | flops 809762816 | bytes 1575940 | tf_op jit(solution)/shard_map/grv,vk->grk/dot_general | solution.py:39
  111.9 6.9 %fusion.7 = f32[1,256,512]{2,1,0:T(8,128)S(1)} fusion(f32[256,512]{1,0:T(8,128)S(1)} %fusion.53, f32[256,512]{1,0:T(8,128)S(1)} %convolution_subtract_fusion.6, f32[256,512]{1,0:T(8,128)S(1)} %convolution_add_fusion.6, f32[]{:T(128)S(6)} %mul.531, f32[512]{0:T(512)S(1)} %fusion.86, f32[256]{0:T(256)S(1)} %get-tuple-element.36), kind=kOutput, calls=%fused_computation.27 | convolution fusion | flops 810024960 | bytes 2100228 | tf_op jit(solution)/shard_map/grv,vk->grk/dot_general | solution.py:39
  123.8 7.9 %fusion.5 = f32[1,256,512]{2,1,0:T(8,128)S(1)} fusion(f32[256,512]{1,0:T(8,128)} %fusion.57, f32[256,512]{1,0:T(8,128)S(1)} %convolution_subtract_fusion.6, f32[256,512]{1,0:T(8,128)S(1)} %convolution_add_fusion.6, f32[]{:T(128)S(6)} %mul.531, f32[512]{0:T(512)S(1)} %fusion.86, f32[256]{0:T(256)S(1)} %get-tuple-element.36), kind=kOutput, calls=%fused_computation.25 | convolution fusion | flops 810024960 | bytes 2100228 | tf_op jit(solution)/shard_map/grv,vk->grk/dot_general | solution.py:39
  150.2 5.9 %fusion.11 = f32[1,512,256]{1,2,0:T(8,128)S(1)} fusion(f32[256,512]{1,0:T(8,128)S(1)} %fusion.51, f32[512,256]{1,0:T(8,128)S(1)} %bitcast.139), kind=kOutput, calls=%fused_computation.31 | convolution fusion | flops 809238528 | bytes 1572864 | tf_op jit(solution)/shard_map/ur,grc->guc/dot_general | solution.py:43
  156.1 6.1 %fusion.9 = f32[1,512,256]{1,2,0:T(8,128)S(1)} fusion(f32[256,512]{1,0:T(8,128)S(1)} %fusion.55, f32[512,256]{1,0:T(8,128)S(1)} %bitcast.125), kind=kOutput, calls=%fused_computation.29 | convolution fusion | flops 809238528 | bytes 1572864 | tf_op jit(solution)/shard_map/ur,grc->guc/dot_general | solution.py:43
  162.2 8.1 %fusion.28 = f32[256,512]{1,0:T(8,128)S(1)} fusion(f32[1,512,256]{1,2,0:T(8,128)S(1)} %fusion.11, f32[1,512,256]{1,2,0:T(8,128)S(1)} %fusion.9, f32[256]{0:T(256)S(1)} %get-tuple-element.37, f32[512]{0:T(512)S(1)} %multiply_multiply_fusion, f32[]{:T(128)} %get-tuple-element.35, f32[]{:T(128)} %get-tuple-element.27), kind=kOutput, calls=%fused_computation.49 | convolution fusion | flops 809893888 | bytes 1575944 | tf_op jit(solution)/shard_map/ur,grc->guc/dot_general | solution.py:43
  170.3 9.3 %fusion.32 = f32[256,512]{1,0:T(8,128)} fusion(f32[1,512,256]{1,2,0:T(8,128)S(1)} %fusion.11, f32[1,512,256]{1,2,0:T(8,128)S(1)} %fusion.9, f32[256]{0:T(256)S(1)} %get-tuple-element.37, f32[512]{0:T(512)S(1)} %multiply_multiply_fusion, f32[]{:T(128)} %get-tuple-element.35, f32[]{:T(128)} %get-tuple-element.27), kind=kOutput, calls=%fused_computation.53 | convolution fusion | flops 809893888 | bytes 1575944 | tf_op jit(solution)/shard_map/ur,grc->guc/dot_general | solution.py:43
  179.6 8.2 %fusion = f32[1,512,256]{1,2,0:T(8,128)S(1)} fusion(f32[256,512]{1,0:T(8,128)S(1)} %fusion.28, f32[1,512,256]{1,2,0:T(8,128)S(1)} %fusion.11, f32[1,512,256]{1,2,0:T(8,128)S(1)} %fusion.9, f32[256]{0:T(256)S(1)} %get-tuple-element.37, f32[512]{0:T(512)S(1)} %multiply_multiply_fusion, f32[]{:T(128)} %get-tuple-element.35, f32[]{:T(128)} %get-tuple-element.27), kind=kOutput, calls=%fused_computation.11 | convolution fusion | flops 810024960 | bytes 2100232 | tf_op jit(solution)/shard_map/ur,grc->guc/dot_general | solution.py:43
  192.5 9.2 %fusion.1 = f32[1,512,256]{1,2,0:T(8,128)S(1)} fusion(f32[256,512]{1,0:T(8,128)} %fusion.32, f32[1,512,256]{1,2,0:T(8,128)S(1)} %fusion.11, f32[1,512,256]{1,2,0:T(8,128)S(1)} %fusion.9, f32[256]{0:T(256)S(1)} %get-tuple-element.37, f32[512]{0:T(512)S(1)} %multiply_multiply_fusion, f32[]{:T(128)} %get-tuple-element.35, f32[]{:T(128)} %get-tuple-element.27), kind=kOutput, calls=%fused_computation.13 | convolution fusion | flops 810024960 | bytes 2100232 | tf_op jit(solution)/shard_map/ur,grc->guc/dot_general | solution.py:43
  219.4 5.9 %convolution_subtract_fusion.2 = f32[256,512]{1,0:T(8,128)S(1)} fusion(f32[256,512]{1,0:T(8,128)S(1)} %fusion.45, f32[256,512]{0,1:T(8,128)S(1)} %bitcast.141), kind=kOutput, calls=%fused_computation.8 | convolution fusion | flops 809107456 | bytes 1572864 | tf_op jit(solution)/shard_map/grv,vk->grk/dot_general | solution.py:39
  225.3 6.3 %convolution_add_fusion.2 = f32[256,512]{1,0:T(8,128)S(1)} fusion(f32[256,512]{1,0:T(8,128)S(1)} %fusion.48, f32[256,512]{0,1:T(8,128)S(1)} %bitcast.127), kind=kOutput, calls=%fused_computation.9 | convolution fusion | flops 809107456 | bytes 1572864 | tf_op jit(solution)/shard_map/grv,vk->grk/dot_general | solution.py:39
  231.6 6.9 %fusion.39 = f32[256,512]{1,0:T(8,128)S(1)} fusion(f32[256,512]{1,0:T(8,128)S(1)} %convolution_subtract_fusion.2, f32[256,512]{1,0:T(8,128)S(1)} %convolution_add_fusion.2, f32[]{:T(128)S(6)} %mul.531, f32[512]{0:T(512)S(1)} %fusion.86, f32[256]{0:T(256)S(1)} %get-tuple-element.36), kind=kOutput, calls=%fused_computation.69 | convolution fusion | flops 809762816 | bytes 1575940 | tf_op jit(solution)/shard_map/grv,vk->grk/dot_general | solution.py:39
  238.4 7.8 %fusion.43 = f32[256,512]{1,0:T(8,128)} fusion(f32[256,512]{1,0:T(8,128)S(1)} %convolution_subtract_fusion.2, f32[256,512]{1,0:T(8,128)S(1)} %convolution_add_fusion.2, f32[]{:T(128)S(6)} %mul.531, f32[512]{0:T(512)S(1)} %fusion.86, f32[256]{0:T(256)S(1)} %get-tuple-element.36), kind=kOutput, calls=%fused_computation.71 | convolution fusion | flops 809762816 | bytes 1575940 | tf_op jit(solution)/shard_map/grv,vk->grk/dot_general | solution.py:39
  246.3 6.9 %fusion.15 = f32[1,256,512]{2,1,0:T(8,128)S(1)} fusion(f32[256,512]{1,0:T(8,128)S(1)} %fusion.39, f32[256,512]{1,0:T(8,128)S(1)} %convolution_subtract_fusion.2, f32[256,512]{1,0:T(8,128)S(1)} %convolution_add_fusion.2, f32[]{:T(128)S(6)} %mul.531, f32[512]{0:T(512)S(1)} %fusion.86, f32[256]{0:T(256)S(1)} %get-tuple-element.36), kind=kOutput, calls=%fused_computation.35 | convolution fusion | flops 810024960 | bytes 2100228 | tf_op jit(solution)/shard_map/grv,vk->grk/dot_general | solution.py:39
  258.0 8.0 %fusion.13 = f32[1,256,512]{2,1,0:T(8,128)S(1)} fusion(f32[256,512]{1,0:T(8,128)} %fusion.43, f32[256,512]{1,0:T(8,128)S(1)} %convolution_subtract_fusion.2, f32[256,512]{1,0:T(8,128)S(1)} %convolution_add_fusion.2, f32[]{:T(128)S(6)} %mul.531, f32[512]{0:T(512)S(1)} %fusion.86, f32[256]{0:T(256)S(1)} %get-tuple-element.36), kind=kOutput, calls=%fused_computation.33 | convolution fusion | flops 810024960 | bytes 2100228 | tf_op jit(solution)/shard_map/grv,vk->grk/dot_general | solution.py:39
  283.7 5.9 %fusion.17 = f32[256,512]{1,0:T(8,128)S(1)} fusion(f32[256,512]{1,0:T(8,128)S(1)} %fusion.41, f32[512,256]{1,0:T(8,128)S(1)} %bitcast.133), kind=kOutput, calls=%fused_computation.37 | convolution fusion | flops 809369600 | bytes 1572864 | tf_op jit(solution)/shard_map/ur,grc->guc/dot_general | solution.py:43
  289.5 6.2 %fusion.21 = f32[512,256]{0,1:T(8,128)S(1)} fusion(f32[256,512]{1,0:T(8,128)S(1)} %fusion.17, f32[256,512]{1,0:T(8,128)S(1)} %fusion.37, f32[512,256]{1,0:T(8,128)S(1)} %bitcast.137), kind=kOutput, calls=%fused_computation.41 | convolution fusion | flops 809500672 | bytes 2097152 | tf_op jit(solution)/shard_map/ur,grc->guc/dot_general | solution.py:43
  297.5 62.7 %reduce-scatter.2.cloned.1.call-done = f32[4,32,256]{2,1,0:T(8,128)} async-done(((f32[4,512,256]{2,1,0:T(8,128)}), f32[4,32,256]{2,1,0:T(8,128)}) %reduce-scatter.2.cloned.1.call-update) | async-done | bytes 131088 | tf_op jit(solution)/shard_map/reduce_scatter | solution.py:127
  (84 shorter events, 125.4 us)
Async XLA Ops:
  6.5 1.3 copy-start
  6.5 10.1 %copy-start.5 = (s32[16]{0:T(128)S(1)}, s32[16]{0:T(128)}, u32[]{:S(2)}) copy-start(s32[16]{0:T(128)} %param.13) | copy-start | bytes 196
  6.5 10.8 %copy-start.1 = (s32[16,2]{0,1:T(2,128)S(1)}, s32[16,2]{0,1:T(2,128)}, u32[]{:S(2)}) copy-start(s32[16,2]{0,1:T(2,128)} %param.12) | copy-start | bytes 388
  6.5 11.4 %copy-start.2 = (f32[9]{0:T(128)S(1)}, f32[9]{0:T(128)}, u32[]{:S(2)}) copy-start(f32[9]{0:T(128)} %param.8) | copy-start | bytes 112
  6.5 13.3 %copy-start.3 = (f32[9]{0:T(128)S(1)}, f32[9]{0:T(128)}, u32[]{:S(2)}) copy-start(f32[9]{0:T(128)} %param.10) | copy-start | bytes 112
  6.5 13.3 %copy-start.4 = (f32[9]{0:T(128)S(1)}, f32[9]{0:T(128)}, u32[]{:S(2)}) copy-start(f32[9]{0:T(128)} %param.9) | copy-start | bytes 112
  9.2 21.7 %all-to-all-start = ((bf16[2,16,1,32,256]{4,3,0,2,1:T(8,128)(2,1)}), bf16[2,16,1,32,256]{4,3,0,2,1:T(8,128)(2,1)S(1)}, u32[]{:S(2)}, u32[]{:S(2)}) async-start(bf16[2,16,1,32,256]{4,3,0,2,1:T(8,128)(2,1)} %bitcast.7), calls=%async_computation | async-start | bytes 1048576 | tf_op jit(solution)/shard_map/all_to_all | solution.py:58
  44.4 16.5 %all-to-all-start.2 = ((f32[1,512,256]{2,0,1:T(1,128)}), f32[1,512,256]{2,0,1:T(1,128)S(1)}, u32[]{:S(2)}, u32[]{:S(2)}) async-start(f32[1,512,256]{2,0,1:T(1,128)} %copy.29), calls=%async_computation.2 | async-start | bytes 1048576 | tf_op jit(solution)/shard_map/all_to_all | solution.py:99
  59.8 4.6 %copy-start.6 = (f32[4]{0:T(128)S(1)}, f32[4]{0:T(128)}, u32[]{:S(2)}) copy-start(f32[4]{0:T(128)} %param.11) | copy-start | bytes 52
  60.8 12.0 %all-to-all-start.1 = ((f32[1,512,256]{2,0,1:T(1,128)}), f32[1,512,256]{2,0,1:T(1,128)S(1)}, u32[]{:S(2)}, u32[]{:S(2)}) async-start(f32[1,512,256]{2,0,1:T(1,128)} %copy.27), calls=%async_computation.1 | async-start | bytes 1048576 | tf_op jit(solution)/shard_map/all_to_all | solution.py:98
  119.9 12.9 %all-to-all-start.4 = ((f32[1,256,512]{1,0,2:T(1,128)}), f32[1,256,512]{1,0,2:T(1,128)S(1)}, u32[]{:S(2)}, u32[]{:S(2)}) async-start(f32[1,256,512]{1,0,2:T(1,128)} %copy.33), calls=%async_computation.4 | async-start | bytes 1048576 | tf_op jit(solution)/shard_map/all_to_all | solution.py:113
  132.8 11.3 %all-to-all-start.3 = ((f32[1,256,512]{1,0,2:T(1,128)}), f32[1,256,512]{1,0,2:T(1,128)S(1)}, u32[]{:S(2)}, u32[]{:S(2)}) async-start(f32[1,256,512]{1,0,2:T(1,128)} %copy.31), calls=%async_computation.3 | async-start | bytes 1048576 | tf_op jit(solution)/shard_map/all_to_all | solution.py:112
  188.8 13.9 %all-to-all-start.6 = ((f32[1,512,256]{2,0,1:T(1,128)}), f32[1,512,256]{2,0,1:T(1,128)S(1)}, u32[]{:S(2)}, u32[]{:S(2)}) async-start(f32[1,512,256]{2,0,1:T(1,128)} %copy.37), calls=%async_computation.6 | async-start | bytes 1048576 | tf_op jit(solution)/shard_map/all_to_all | solution.py:99
  202.8 10.5 %all-to-all-start.5 = ((f32[1,512,256]{2,0,1:T(1,128)}), f32[1,512,256]{2,0,1:T(1,128)S(1)}, u32[]{:S(2)}, u32[]{:S(2)}) async-start(f32[1,512,256]{2,0,1:T(1,128)} %copy.35), calls=%async_computation.5 | async-start | bytes 1048576 | tf_op jit(solution)/shard_map/all_to_all | solution.py:98
  254.3 12.7 %all-to-all-start.8 = ((f32[1,256,512]{1,0,2:T(1,128)}), f32[1,256,512]{1,0,2:T(1,128)S(1)}, u32[]{:S(2)}, u32[]{:S(2)}) async-start(f32[1,256,512]{1,0,2:T(1,128)} %copy.41), calls=%async_computation.8 | async-start | bytes 1048576 | tf_op jit(solution)/shard_map/all_to_all | solution.py:113
  267.0 10.6 %all-to-all-start.7 = ((f32[1,256,512]{1,0,2:T(1,128)}), f32[1,256,512]{1,0,2:T(1,128)S(1)}, u32[]{:S(2)}, u32[]{:S(2)}) async-start(f32[1,256,512]{1,0,2:T(1,128)} %copy.39), calls=%async_computation.7 | async-start | bytes 1048576 | tf_op jit(solution)/shard_map/all_to_all | solution.py:112
  270.5 89.7 %reduce-scatter.2.cloned.1.call-start = ((), (), s32[]{:S(2)}) async-start(), calls=%async_computation.10 | async-start | bytes 2228224 | tf_op jit(solution)/shard_map/reduce_scatter | solution.py:127
Sparse Core Ops, SparseCore 0:
  297.7 62.4 reduce-scatter.1
where the time goes:
time: 375 us; the launch traced here: 369 us
  matrix products  213 us (57%)
  waiting for transfers between devices  79 us (21%)
  starting transfers between devices  37 us (10%)
  between operations  16.3 us (4%)
  local copies, waits for them, and re-layouts  13.7 us (4%)
  other arithmetic  10.6 us (3%)
    dot_general x16, matrix products, along_last(): jnp.einsum('grv,vk->grk', values, table, precision=lax.Precision.HIGHEST)  107 us
    dot_general x16, matrix products, along_rows(): jnp.einsum('ur,grc->guc', table, values, precision=lax.Precision.HIGHEST)  105 us
    reduce_scatter x1, waiting for transfers between devices, local(): lax.psum_scatter(case_terms, 'path', scatter_dimension=1, tiled=True)  62.7 us
    all_to_all x1, waiting for transfers between devices, local(): lax.all_to_all(picked, 'path', split_axis=1, concat_axis=3, tiled=True)  8.99 us
    all_to_all x2, starting transfers between devices, propagate(): lax.all_to_all(imag_part, 'row', split_axis=2, concat_axis=1, tiled=True)  7.59 us
  transfers between devices with their start and end apart: 10, of which 5 were waited for; matrix products, arithmetic and copies ran while one was open for 18% of the time, Pallas kernels for 0%

commit v1 on v0

v1 whole, which is shorter than its diff:
```python
import functools

import jax
import jax.numpy as jnp
import numpy as np
from jax import lax
from jax.experimental import pallas as pl
from jax.experimental.pallas import tpu as pltpu
from jax.sharding import PartitionSpec as P

CASES = 4
SURF = 9

spread_scale = 2000.0

BF16 = jnp.bfloat16
F32 = jnp.float32
MESH = pl.DeviceIdType.MESH
SMEM = pl.BlockSpec(memory_space=pltpu.SMEM)
VMEM = pl.BlockSpec(memory_space=pltpu.VMEM)

TURN = 2.0 * np.pi
TURN_1 = float(np.float32(6.28125))
TURN_2 = float(np.float32(TURN - 6.28125))


def halves(values):
    high = values.astype(BF16)
    return high, (values - high.astype(F32)).astype(BF16)


def cosine_table(cells):
    counter = np.arange(cells, dtype=np.int64)
    exact = np.cos(TURN / cells * (counter[:, None] * counter[None, :] % cells)) / cells
    high = exact.astype(np.float32).astype(jnp.bfloat16)
    low = (exact - high.astype(np.float64)).astype(np.float32).astype(jnp.bfloat16)
    return np.stack([high, low])


def dot(left, right):
    return jnp.dot(left, right, preferred_element_type=F32)


def dot3(left_high, left_low, right_high, right_low):
    return dot(left_high, right_high) + dot(left_high, right_low) + dot(left_low, right_high)


def cos_sin(phase):
    turns = jnp.floor(phase * (1.0 / TURN) + 0.5)
    rest = (phase - turns * TURN_1) - turns * TURN_2
    return jnp.cos(rest), jnp.sin(rest)


def ghost_scalars(reflect, curvature, position, wave, pair, case, ghost):
    start, turn = pair[ghost, 0], pair[ghost, 1]
    coefficient = spread_scale * wave[case[ghost]] * (position[start] - position[turn])
    return coefficient, curvature[turn], reflect[start] * reflect[turn]


def build_operator(cells, coefficient, power, table, spread, screened, both):
    counter = lax.broadcasted_iota(jnp.int32, (16, cells), 1)
    row = lax.broadcasted_iota(jnp.int32, (16, cells), 0)
    shifted = ((counter + cells // 2) % cells - cells // 2).astype(F32)
    cosine, sine = cos_sin(coefficient * (shifted * shifted / float(cells * cells)))
    transfer = jnp.where(row == 0, cosine, jnp.where(row == 1, -sine, 0.0))
    high, low = halves(transfer)
    kernel_rows = dot3(high, low, table[0], table[1])
    centred = (counter - cells // 2).astype(F32) / float(cells)
    screen_cos, screen_sin = cos_sin(power * (centred * centred))
    screen_cos, screen_sin = screen_cos[0:1], screen_sin[0:1]
    step = 128
    for begin in range(0, cells, step):
        rows = pl.ds(begin, step)
        real, imag = (
            pltpu.roll(
                jnp.broadcast_to(kernel_rows[part : part + 1], (step, cells)),
                begin, 1, stride=1, stride_axis=0,
            )
            for part in (0, 1)
        )
        spread[0, rows, :], spread[1, rows, :] = halves(real)
        spread[2, rows, :], spread[3, rows, :] = halves(imag)
        screened[0, rows, :], screened[1, rows, :] = halves(real * screen_cos - imag * screen_sin)
        screened[2, rows, :], screened[3, rows, :] = halves(real * screen_sin + imag * screen_cos)

    wide = cells // 2

    @pl.loop(0, 2)
    def _(chunk):
        rows = pl.ds(pl.multiple_of(chunk * wide, wide), wide)
        left = [screened[k, rows, :] for k in range(4)]
        right = [spread[k] for k in range(4)]
        real = dot3(left[0], left[1], right[0], right[1]) - dot3(left[2], left[3], right[2], right[3])
        both[0, rows, :], both[1, rows, :] = halves(real)
        imag = dot3(left[0], left[1], right[2], right[3]) + dot3(left[2], left[3], right[0], right[1])
        both[2, rows, :], both[3, rows, :] = halves(imag)


def slab_first(real, imag, slab, both, middle, rows):
    weights = [both[k, :, slab] for k in range(4)]
    new_real = (
        dot(real, weights[0]) + dot(real, weights[1]) - dot(imag, weights[2]) - dot(imag, weights[3])
    )
    middle[0, rows, :], middle[1, rows, :] = halves(new_real)
    new_imag = (
        dot(real, weights[2]) + dot(real, weights[3]) + dot(imag, weights[0]) + dot(imag, weights[1])
    )
    middle[2, rows, :], middle[3, rows, :] = halves(new_imag)


def slab_second(both, middle, rows, power):
    left = [both[k, rows, :] for k in range(4)]
    right = [middle[k] for k in range(4)]
    real = dot3(left[0], left[1], right[0], right[1]) - dot3(left[2], left[3], right[2], right[3])
    imag = dot3(left[0], left[1], right[2], right[3]) + dot3(left[2], left[3], right[0], right[1])
    return power * (real * real + imag * imag)


def scratch_of(cells, slab_cells):
    return [
        pltpu.VMEM((4, cells, cells), BF16),
        pltpu.VMEM((4, cells, cells), BF16),
        pltpu.VMEM((4, cells, cells), BF16),
        pltpu.VMEM((4, cells, slab_cells), BF16),
    ]


def whole_kernel(
    cells, paths, row_count,
    field, table_hbm, reflect, curvature, position, wave, pair, case, out,
    spread, screened, both, middle, table, outgoing, held, bright, got,
    table_sem, send_sem, recv_sem, pass_send, pass_recv, out_send, out_recv,
):
    path, row = lax.axis_index("path"), lax.axis_index("row")
    chip, slab_id = path // row_count, path % row_count
    own = chip * row_count + row
    ghosts = pair.shape[0]
    slab_cells = cells // row_count
    piece = cells // paths
    devices = paths * row_count
    mine = path * row_count + row
    is_home = slab_id == row

    barrier = pltpu.get_barrier_semaphore()

    @pl.loop(1, devices)
    def _(step):
        other = (mine + step) % devices
        pl.semaphore_signal(
            barrier, inc=1, device_id=(other // row_count, other % row_count), device_id_type=MESH
        )

    load_table = pltpu.make_async_copy(table_hbm, table, table_sem)
    load_table.start()

    @pl.loop(0, ghosts)
    def _(ghost):
        index = case[ghost] * SURF + pair[ghost, 0]
        outgoing[ghost, 0] = field[0, index]
        outgoing[ghost, 1] = field[1, index]

    pl.semaphore_wait(barrier, devices - 1)

    def field_copy(ghost):
        return pltpu.make_async_remote_copy(
            src_ref=outgoing.at[ghost],
            dst_ref=held.at[row, path],
            send_sem=send_sem.at[ghost],
            recv_sem=recv_sem.at[path],
            device_id=((ghost // row_count) * row_count + row, ghost % row_count),
            device_id_type=MESH,
        )

    def field_arrival(source):
        return pltpu.make_async_remote_copy(
            src_ref=outgoing.at[0],
            dst_ref=held.at[slab_id, source],
            send_sem=send_sem.at[0],
            recv_sem=recv_sem.at[source],
            device_id=(path, row),
            device_id_type=MESH,
        )

    home_copy = pltpu.make_async_copy(outgoing.at[own], held.at[row, path], recv_sem.at[path])

    @pl.loop(0, ghosts)
    def _(step):
        ghost = (own + ghosts // 2 + step) % ghosts

        @pl.when(jnp.logical_or(ghost != own, jnp.logical_not(is_home)))
        def _():
            field_copy(ghost).start()

    @pl.when(is_home)
    def _():
        home_copy.start()

    load_table.wait()
    coefficient, power, gain = ghost_scalars(
        reflect, curvature, position, wave, pair, case, own
    )
    build_operator(cells, coefficient, power, table, spread, screened, both)

    def pass_copy(source, turn):
        return pltpu.make_async_remote_copy(
            src_ref=held.at[slab_id, source],
            dst_ref=held.at[slab_id, source],
            send_sem=pass_send.at[turn - 1, source],
            recv_sem=pass_recv.at[turn - 1, source],
            device_id=(chip * row_count + (slab_id + turn) % row_count, row),
            device_id_type=MESH,
        )

    def pass_arrival(source, turn):
        return pltpu.make_async_remote_copy(
            src_ref=held.at[slab_id, source],
            dst_ref=held.at[(slab_id + row_count - turn) % row_count, source],
            send_sem=pass_send.at[turn - 1, source],
            recv_sem=pass_recv.at[turn - 1, source],
            device_id=(path, row),
            device_id_type=MESH,
        )

    @pl.loop(0, paths)
    def _(step):
        source = (path + step) % paths

        @pl.when(jnp.logical_or(source != path, jnp.logical_not(is_home)))
        def _():
            field_arrival(source).wait_recv()

        @pl.when(jnp.logical_and(source == path, is_home))
        def _():
            home_copy.wait()

        for turn in range(1, row_count):
            pass_copy(source, turn).start()

    @pl.loop(0, paths)
    def _(source):
        for turn in range(1, row_count):
            pass_arrival(source, turn).wait_recv()

    slab = pl.ds(pl.multiple_of(slab_id * slab_cells, slab_cells), slab_cells)
    parts = 2
    group = paths // parts
    tall = cells // parts

    @pl.loop(0, parts)
    def _(chunk):
        def rows_of(part):
            return jnp.concatenate(
                [
                    held[side, pl.ds(chunk * group, group), part].reshape(tall, slab_cells)
                    for side in range(row_count)
                ],
                axis=1,
            )

        slab_first(
            rows_of(0), rows_of(1), slab, both, middle, pl.ds(pl.multiple_of(chunk * tall, tall), tall)
        )

    def bright_copy(target):
        return pltpu.make_async_remote_copy(
            src_ref=bright.at[target],
            dst_ref=got.at[own],
            send_sem=out_send.at[target],
            recv_sem=out_recv.at[own],
            device_id=(target, slab_id),
            device_id_type=MESH,
        )

    def bright_arrival(ghost):
        return pltpu.make_async_remote_copy(
            src_ref=bright.at[0],
            dst_ref=got.at[ghost],
            send_sem=out_send.at[0],
            recv_sem=out_recv.at[ghost],
            device_id=(path, row),
            device_id_type=MESH,
        )

    home_bright = pltpu.make_async_copy(bright.at[path], got.at[own], out_recv.at[own])

    @pl.loop(0, parts)
    def _(turn):
        chunk = (path // group + 1 + turn) % parts
        rows = pl.ds(pl.multiple_of(chunk * tall, tall), tall)
        intensity = slab_second(both, middle, rows, gain * gain * (CASES / ghosts))
        bright[pl.ds(chunk * group, group)] = intensity.reshape(group, piece, slab_cells)

        @pl.loop(0, group)
        def _(step):
            target = chunk * group + (path + step) % group

            @pl.when(jnp.logical_or(target != path, jnp.logical_not(is_home)))
            def _():
                bright_copy(target).start()

            @pl.when(jnp.logical_and(target == path, is_home))
            def _():
                home_bright.start()

    out[...] = jnp.zeros_like(out)

    @pl.loop(0, ghosts)
    def _(step):
        ghost = (own + step) % ghosts

        @pl.when(jnp.logical_or(ghost != own, jnp.logical_not(is_home)))
        def _():
            bright_arrival(ghost).wait_recv()

        @pl.when(jnp.logical_and(ghost == own, is_home))
        def _():
            home_bright.wait()

        values = got[ghost]
        for index in range(CASES):
            chosen = jnp.where(case[ghost] == index, 1.0, 0.0)
            out[index] += chosen * values

    @pl.loop(0, ghosts)
    def _(ghost):
        @pl.when(jnp.logical_or(ghost != own, jnp.logical_not(is_home)))
        def _():
            field_copy(ghost).wait_send()

    @pl.loop(0, paths)
    def _(source):
        for turn in range(1, row_count):
            pass_copy(source, turn).wait_send()

        @pl.when(jnp.logical_or(source != path, jnp.logical_not(is_home)))
        def _():
            bright_copy(source).wait_send()


def whole(cells, paths, row_count, main_field, table, *small):
    ghosts = small[-1].shape[0]
    piece, slab_cells = cells // paths, cells // row_count
    return pl.pallas_call(
        functools.partial(whole_kernel, cells, paths, row_count),
        out_shape=jax.ShapeDtypeStruct((CASES, piece, slab_cells), F32),
        in_specs=[VMEM, pl.BlockSpec(memory_space=pl.ANY)] + [SMEM] * 6,
        out_specs=VMEM,
        scratch_shapes=scratch_of(cells, slab_cells)
        + [
            pltpu.VMEM((2, cells, cells), BF16),
            pltpu.VMEM((ghosts, 2, piece, slab_cells), BF16),
            pltpu.VMEM((row_count, paths, 2, piece, slab_cells), BF16),
            pltpu.VMEM((paths, piece, slab_cells), F32),
            pltpu.VMEM((ghosts, piece, slab_cells), F32),
            pltpu.SemaphoreType.DMA(()),
            pltpu.SemaphoreType.DMA((ghosts,)),
            pltpu.SemaphoreType.DMA((paths,)),
            pltpu.SemaphoreType.DMA((row_count - 1, paths)),
            pltpu.SemaphoreType.DMA((row_count - 1, paths)),
            pltpu.SemaphoreType.DMA((paths,)),
            pltpu.SemaphoreType.DMA((ghosts,)),
        ],
        compiler_params=pltpu.CompilerParams(
            collective_id=0, has_side_effects=True, vmem_limit_bytes=48 * 1024 * 1024
        ),
    )(main_field, table, *small)


def slab_kernel(
    cells, row_count, field, table, reflect, curvature, position, wave, pair, case, slot, out,
    spread, screened, both, middle,
):
    slab_cells = cells // row_count
    coefficient, power, gain = ghost_scalars(
        reflect, curvature, position, wave, pair, case, slot[0]
    )
    build_operator(cells, coefficient, power, table, spread, screened, both)
    slab = pl.ds(pl.multiple_of(slot[1] * slab_cells, slab_cells), slab_cells)
    tall = cells // 2

    @pl.loop(0, 2)
    def _(chunk):
        rows = pl.ds(pl.multiple_of(chunk * tall, tall), tall)
        slab_first(field[0, rows, :], field[1, rows, :], slab, both, middle, rows)

    @pl.loop(0, 2)
    def _(chunk):
        rows = pl.ds(pl.multiple_of(chunk * tall, tall), tall)
        out[rows, :] = slab_second(both, middle, rows, gain * gain)


def local(main_field, table, *small):
    paths = lax.axis_size("path")
    row_count = lax.axis_size("row")
    piece, slab_cells = main_field.shape[2:]
    cells = piece * paths
    pair, case = small[-2:]
    ghosts = pair.shape[0]
    if piece % 16 == 0 and ghosts == paths and paths % (2 * row_count) == 0 and row_count > 1:
        return whole(cells, paths, row_count, main_field, table, *small)
    per_device = ghosts // paths
    picked = main_field[:, case * SURF + pair[:, 0]]
    picked = picked.reshape(2, paths, per_device, piece, slab_cells)
    arrived = lax.all_to_all(picked, "path", split_axis=1, concat_axis=3, tiled=True)
    fields = lax.all_gather(
        arrived.reshape(2, per_device, cells, slab_cells), "row", axis=3, tiled=True
    )
    bright = []
    for index in range(per_device):
        slot = jnp.stack([lax.axis_index("path") * per_device + index, lax.axis_index("row")])
        bright.append(
            pl.pallas_call(
                functools.partial(slab_kernel, cells, row_count),
                out_shape=jax.ShapeDtypeStruct((cells, slab_cells), F32),
                in_specs=[VMEM, VMEM] + [SMEM] * 7,
                out_specs=VMEM,
                scratch_shapes=scratch_of(cells, slab_cells),
                compiler_params=pltpu.CompilerParams(vmem_limit_bytes=48 * 1024 * 1024),
            )(fields[:, index], table, *small, slot)
        )
    got = lax.all_to_all(jnp.stack(bright), "path", split_axis=1, concat_axis=0, tiled=True)
    got = got.reshape(paths, per_device, piece, slab_cells).reshape(ghosts, piece, slab_cells)
    chosen = (case[:, None] == jnp.arange(CASES, dtype=jnp.int32)).astype(F32)
    total = jnp.sum(chosen[:, :, None, None] * got[:, None], 0)
    return total * (CASES / ghosts)


def solution(mesh):
    in_specs = (P(None, None, "path", "row"), P(), P(), P(), P(), P(), P())
    out_specs = P(None, "path", "row")

    def run(main_field, *small):
        table = cosine_table(main_field.shape[2] * mesh.shape["path"])
        return local(main_field, jnp.asarray(table), *small)

    return jax.shard_map(run, mesh=mesh, in_specs=in_specs, out_specs=out_specs, check_vma=False)
```

time: 375 us -> 46.3 us (0.12); the launches traced: 369 us -> 46 us
  matrix products: 213 us -> 0 us
  waiting for transfers between devices: 79 us -> 0 us
  Pallas kernels: 0 us -> 38.8 us
  starting transfers between devices: 37 us -> 0 us
  between operations: 16.3 us -> 0.02 us
  other arithmetic: 10.6 us -> 0 us
  local copies, waits for them, and re-layouts: 13.7 us -> 7.18 us
    dot_general x32 -> x0, matrix products: 213 us -> none  [the longest x16 107 us: along_last(): jnp.einsum('grv,vk->grk', values, table, precision=lax.Precision.HIGHEST)]
    reduce_scatter x1 -> x0, waiting for transfers between devices: 62.7 us -> none  [local(): lax.psum_scatter(case_terms, 'path', scatter_dimension=1, tiled=True)]
    pallas_call x0 -> x1, Pallas kernels: none -> 38.8 us  [whole(): pl.pallas_call(functools.partial(whole_kernel, cells, paths, row_count),...]
    all_to_all x9 -> x0, starting transfers between devices: 36.7 us -> none  [the longest x2 7.59 us: propagate(): lax.all_to_all(imag_part, 'row', split_axis=2, concat_axis=1, tiled=True)]
    all_to_all x9 -> x0, waiting for transfers between devices: 16.4 us -> none  [the longest x1 8.99 us: local(): lax.all_to_all(picked, 'path', split_axis=1, concat_axis=3, tiled=True)]
    unnamed x22 -> x16, local copies, waits for them, and re-layouts: 0.8 us -> 7.18 us
    reduce_sum x3 -> x0, other arithmetic: 5.22 us -> none  [the longest x1 2.01 us: local(): jnp.sum(turn_hot * position[None, :], 1)]
    div x4 -> x0, local copies, waits for them, and re-layouts: 4.21 us -> none  [the longest x2 2.1 us: complex_apply(): (contract(imag_part, cosine_table) + contract(real_part, sine_table)) / f...]
  transfers between devices with their start and end apart: 10 -> 0, of which waited for: 5 -> 0; matrix products, arithmetic and copies ran while one was open for 18% -> 0% of each run, Pallas kernels for 0% -> 0%
where the time goes in v1:
time: 46.3 us; the launch traced here: 46 us
  Pallas kernels  38.8 us (84%)
  local copies, waits for them, and re-layouts  7.18 us (16%)
    pallas_call x1, Pallas kernels, whole(): pl.pallas_call(functools.partial(whole_kernel, cells, paths, row_count),...  38.8 us
    unnamed x16, local copies, waits for them, and re-layouts  7.18 us

profile of v1, /device:TPU:0, one launch (start us, length us, event | category | flops | bytes accessed | tf_op | source)
XLA Modules:
  0.0 46.0 jit_solution(15480613025954837172)
XLA Ops:
  0.0 0.8 %copy.9.pair = s32[16,2]{1,0:T(8,128)S(1)} copy(s32[16,2]{0,1:T(2,128)} %param.13) | data formatting | bytes 256 | tf_op args[5]
  0.8 0.0 copy-start
  0.8 1.3 %copy-done = bf16[2,36,32,256]{3,2,1,0:T(8,128)(2,1)S(1)} copy-done((bf16[2,36,32,256]{3,2,1,0:T(8,128)(2,1)S(1)}, bf16[2,36,32,256]{3,2,1,0:T(8,128)(2,1)}, u32[]{:S(2)}) %copy-start) | copy-done | bytes 1179672
  2.0 0.0 copy-start.1
  2.0 1.2 %copy-done.1 = bf16[2,512,512]{2,1,0:T(8,128)(2,1)S(1)} copy-done((bf16[2,512,512]{2,1,0:T(8,128)(2,1)S(1)}, bf16[2,512,512]{2,1,0:T(8,128)(2,1)}, u32[]{:S(2)}) %copy-start.1) | copy-done | bytes 1048600
  3.3 0.0 copy-start.2
  3.3 0.7 %copy-done.2 = f32[9]{0:T(128)S(1)} copy-done((f32[9]{0:T(128)S(1)}, f32[9]{0:T(128)}, u32[]{:S(2)}) %copy-start.2) | copy-done | bytes 60
  3.9 0.0 copy-start.3
  3.9 0.7 %copy-done.3 = f32[9]{0:T(128)S(1)} copy-done((f32[9]{0:T(128)S(1)}, f32[9]{0:T(128)}, u32[]{:S(2)}) %copy-start.3) | copy-done | bytes 60
  4.6 0.0 copy-start.4
  4.6 0.7 %copy-done.4 = f32[9]{0:T(128)S(1)} copy-done((f32[9]{0:T(128)S(1)}, f32[9]{0:T(128)}, u32[]{:S(2)}) %copy-start.4) | copy-done | bytes 60
  5.2 0.0 copy-start.5
  5.2 0.7 %copy-done.5 = f32[4]{0:T(128)S(1)} copy-done((f32[4]{0:T(128)S(1)}, f32[4]{0:T(128)}, u32[]{:S(2)}) %copy-start.5) | copy-done | bytes 40
  5.9 0.0 copy-start.6
  5.9 0.7 %copy-done.6 = s32[16]{0:T(128)S(1)} copy-done((s32[16]{0:T(128)S(1)}, s32[16]{0:T(128)}, u32[]{:S(2)}) %copy-start.6) | copy-done | bytes 88
  6.5 38.8 %shard_map.82 = f32[4,32,256]{2,1,0:T(8,128)S(1)} custom-call(bf16[2,36,32,256]{3,2,1,0:T(8,128)(2,1)S(1)} %copy-done, bf16[2,512,512]{2,1,0:T(8,128)(2,1)S(1)} %copy-done.1, f32[9]{0:T(128)S(1)} %copy-done.2, f32[9]{0:T(128)S(1)} %copy-done.3, f32[9]{0:T(128)S(1)} %copy-done.4, f32[4]{0:T(128)S(1)} %copy-done.5, s32[16,2]{1,0:T(8,128)S(1)} %copy.9.pair, ...), custom_call_target="tpu_custom_call" | custom-call | tf_op jit(solution)/shard_map/pallas_call | solution.py:343
  45.4 0.7 %copy.11 = f32[4,32,256]{2,1,0:T(8,128)} copy(f32[4,32,256]{2,1,0:T(8,128)S(1)} %shard_map.82) | data formatting | bytes 262144
Async XLA Ops:
  0.8 1.3 %copy-start = (bf16[2,36,32,256]{3,2,1,0:T(8,128)(2,1)S(1)}, bf16[2,36,32,256]{3,2,1,0:T(8,128)(2,1)}, u32[]{:S(2)}) copy-start(bf16[2,36,32,256]{3,2,1,0:T(8,128)(2,1)} %field.1) | copy-start | bytes 3538948
  2.0 1.2 %copy-start.1 = (bf16[2,512,512]{2,1,0:T(8,128)(2,1)S(1)}, bf16[2,512,512]{2,1,0:T(8,128)(2,1)}, u32[]{:S(2)}) copy-start(bf16[2,512,512]{2,1,0:T(8,128)(2,1)} %constant.2.clone.table_hbm) | copy-start | bytes 3145732
  3.3 0.7 %copy-start.2 = (f32[9]{0:T(128)S(1)}, f32[9]{0:T(128)}, u32[]{:S(2)}) copy-start(f32[9]{0:T(128)} %reflect.1) | copy-start | bytes 112
  3.9 0.7 %copy-start.3 = (f32[9]{0:T(128)S(1)}, f32[9]{0:T(128)}, u32[]{:S(2)}) copy-start(f32[9]{0:T(128)} %curvature.1) | copy-start | bytes 112
  4.6 0.7 %copy-start.4 = (f32[9]{0:T(128)S(1)}, f32[9]{0:T(128)}, u32[]{:S(2)}) copy-start(f32[9]{0:T(128)} %position.1) | copy-start | bytes 112
  5.2 0.7 %copy-start.5 = (f32[4]{0:T(128)S(1)}, f32[4]{0:T(128)}, u32[]{:S(2)}) copy-start(f32[4]{0:T(128)} %wave.1) | copy-start | bytes 52
  5.9 0.7 %copy-start.6 = (s32[16]{0:T(128)S(1)}, s32[16]{0:T(128)}, u32[]{:S(2)}) copy-start(s32[16]{0:T(128)} %case.1) | copy-start | bytes 196

commit v2 on v1

--- a/solution.py
+++ b/solution.py
@@ -52,7 +52,7 @@
 
 
 def ghost_scalars(reflect, curvature, position, wave, pair, case, ghost):
-    start, turn = pair[ghost, 0], pair[ghost, 1]
+    start, turn = pair[0, ghost], pair[1, ghost]
     coefficient = spread_scale * wave[case[ghost]] * (position[start] - position[turn])
     return coefficient, curvature[turn], reflect[start] * reflect[turn]
 
@@ -127,20 +127,35 @@
 
 def whole_kernel(
     cells, paths, row_count,
-    field, table_hbm, reflect, curvature, position, wave, pair, case, out,
-    spread, screened, both, middle, table, outgoing, held, bright, got,
-    table_sem, send_sem, recv_sem, pass_send, pass_recv, out_send, out_recv,
+    field_hbm, table_hbm, *rest,
 ):
+    small_hbm, (out, spread, screened, both, middle, field, table, *small), rest = (
+        rest[:6], rest[6:19], rest[19:]
+    )
+    (
+        outgoing, held, bright, got,
+        load_sem, send_sem, recv_sem, pass_send, pass_recv, out_send, out_recv,
+    ) = rest
+    reflect, curvature, position, wave, pair, case = small
     path, row = lax.axis_index("path"), lax.axis_index("row")
     chip, slab_id = path // row_count, path % row_count
     own = chip * row_count + row
-    ghosts = pair.shape[0]
+    ghosts = case.shape[0]
     slab_cells = cells // row_count
     piece = cells // paths
     devices = paths * row_count
     mine = path * row_count + row
     is_home = slab_id == row
 
+    loads = [
+        pltpu.make_async_copy(source, target, load_sem.at[index])
+        for index, (source, target) in enumerate(
+            zip((field_hbm, table_hbm, *small_hbm), (field, table, *small))
+        )
+    ]
+    for load in loads[2:] + loads[:2]:
+        load.start()
+
     barrier = pltpu.get_barrier_semaphore()
 
     @pl.loop(1, devices)
@@ -150,12 +165,12 @@
             barrier, inc=1, device_id=(other // row_count, other % row_count), device_id_type=MESH
         )
 
-    load_table = pltpu.make_async_copy(table_hbm, table, table_sem)
-    load_table.start()
+    for load in loads[2:] + loads[:1]:
+        load.wait()
 
     @pl.loop(0, ghosts)
     def _(ghost):
-        index = case[ghost] * SURF + pair[ghost, 0]
+        index = case[ghost] * SURF + pair[0, ghost]
         outgoing[ghost, 0] = field[0, index]
         outgoing[ghost, 1] = field[1, index]
 
@@ -195,7 +210,7 @@
     def _():
         home_copy.start()
 
-    load_table.wait()
+    loads[1].wait()
     coefficient, power, gain = ghost_scalars(
         reflect, curvature, position, wave, pair, case, own
     )
@@ -343,16 +358,18 @@
     return pl.pallas_call(
         functools.partial(whole_kernel, cells, paths, row_count),
         out_shape=jax.ShapeDtypeStruct((CASES, piece, slab_cells), F32),
-        in_specs=[VMEM, pl.BlockSpec(memory_space=pl.ANY)] + [SMEM] * 6,
+        in_specs=[pl.BlockSpec(memory_space=pltpu.HBM)] * 8,
         out_specs=VMEM,
         scratch_shapes=scratch_of(cells, slab_cells)
         + [
+            pltpu.VMEM(main_field.shape, BF16),
             pltpu.VMEM((2, cells, cells), BF16),
+            *[pltpu.SMEM(array.shape, array.dtype) for array in small],
             pltpu.VMEM((ghosts, 2, piece, slab_cells), BF16),
             pltpu.VMEM((row_count, paths, 2, piece, slab_cells), BF16),
             pltpu.VMEM((paths, piece, slab_cells), F32),
             pltpu.VMEM((ghosts, piece, slab_cells), F32),
-            pltpu.SemaphoreType.DMA(()),
+            pltpu.SemaphoreType.DMA((8,)),
             pltpu.SemaphoreType.DMA((ghosts,)),
             pltpu.SemaphoreType.DMA((paths,)),
             pltpu.SemaphoreType.DMA((row_count - 1, paths)),
@@ -361,7 +378,7 @@
             pltpu.SemaphoreType.DMA((ghosts,)),
         ],
         compiler_params=pltpu.CompilerParams(
-            collective_id=0, has_side_effects=True, vmem_limit_bytes=48 * 1024 * 1024
+            collective_id=0, has_side_effects=True, vmem_limit_bytes=60 * 1024 * 1024
         ),
     )(main_field, table, *small)
 
@@ -395,11 +412,11 @@
     piece, slab_cells = main_field.shape[2:]
     cells = piece * paths
     pair, case = small[-2:]
-    ghosts = pair.shape[0]
+    ghosts = case.shape[0]
     if piece % 16 == 0 and ghosts == paths and paths % (2 * row_count) == 0 and row_count > 1:
         return whole(cells, paths, row_count, main_field, table, *small)
     per_device = ghosts // paths
-    picked = main_field[:, case * SURF + pair[:, 0]]
+    picked = main_field[:, case * SURF + pair[0]]
     picked = picked.reshape(2, paths, per_device, piece, slab_cells)
     arrived = lax.all_to_all(picked, "path", split_axis=1, concat_axis=3, tiled=True)
     fields = lax.all_gather(
@@ -429,7 +446,8 @@
     in_specs = (P(None, None, "path", "row"), P(), P(), P(), P(), P(), P())
     out_specs = P(None, "path", "row")
 
-    def run(main_field, *small):
+    def run(main_field, reflect, curvature, position, wave, pair, case):
+        small = (reflect, curvature, position, wave, pair.T, case)
         table = cosine_table(main_field.shape[2] * mesh.shape["path"])
         return local(main_field, jnp.asarray(table), *small)
 

time: 46.3 us -> 40.5 us (0.87)
  local copies, waits for them, and re-layouts: 7.18 us -> 1.57 us
    unnamed x16 -> x1, local copies, waits for them, and re-layouts: 7.18 us -> 1.57 us
where the time goes in v2:
time: 40.5 us; the launch traced here: 40.3 us
  Pallas kernels  38.7 us (96%)
  local copies, waits for them, and re-layouts  1.57 us (4%)
    pallas_call x1, Pallas kernels, whole(): pl.pallas_call(functools.partial(whole_kernel, cells, paths, row_count),...  38.7 us
    unnamed x1, local copies, waits for them, and re-layouts  1.57 us

profile of v2, /device:TPU:0, one launch (start us, length us, event | category | flops | bytes accessed | tf_op | source)
XLA Modules:
  0.0 40.3 jit_solution(14209876007680551618)
XLA Ops:
  0.0 38.7 %shard_map.82 = f32[4,32,256]{2,1,0:T(8,128)} custom-call(bf16[2,36,32,256]{3,2,1,0:T(8,128)(2,1)} %field_hbm.1, bf16[2,512,512]{2,1,0:T(8,128)(2,1)} %constant.2.clone.table_hbm, f32[9]{0:T(128)} %rest_0_.1, f32[9]{0:T(128)} %rest_1_.1, f32[9]{0:T(128)} %rest_2_.1, f32[4]{0:T(128)} %rest_3_.1, s32[2,16]{1,0:T(2,128)} %bitcast.1, s32[16]{0:T(128)} %rest_5_.1), custom_call_target="tpu_custom_call" | custom-call | tf_op jit(solution)/shard_map/pallas_call | solution.py:358
  38.7 1.6 %copy.10 = f32[4,32,256]{2,1,0:T(8,128)} copy(f32[4,32,256]{2,1,0:T(8,128)} %shard_map.82) | data formatting | bytes 262144

commit v3 on v2

--- a/solution.py
+++ b/solution.py
@@ -200,7 +200,9 @@
 
     @pl.loop(0, ghosts)
     def _(step):
-        ghost = (own + ghosts // 2 + step) % ghosts
+        part = ghosts // 2
+        turned = (own + step) % part
+        ghost = jnp.where(step >= part, (turned + 3 * (ghosts // 4)) % ghosts, turned + ghosts // 4)
 
         @pl.when(jnp.logical_or(ghost != own, jnp.logical_not(is_home)))
         def _():
@@ -236,33 +238,35 @@
             device_id_type=MESH,
         )
 
-    @pl.loop(0, paths)
-    def _(step):
-        source = (path + step) % paths
-
-        @pl.when(jnp.logical_or(source != path, jnp.logical_not(is_home)))
-        def _():
-            field_arrival(source).wait_recv()
-
-        @pl.when(jnp.logical_and(source == path, is_home))
-        def _():
-            home_copy.wait()
-
-        for turn in range(1, row_count):
-            pass_copy(source, turn).start()
-
-    @pl.loop(0, paths)
-    def _(source):
-        for turn in range(1, row_count):
-            pass_arrival(source, turn).wait_recv()
-
     slab = pl.ds(pl.multiple_of(slab_id * slab_cells, slab_cells), slab_cells)
     parts = 2
     group = paths // parts
     tall = cells // parts
 
     @pl.loop(0, parts)
-    def _(chunk):
+    def _(turned):
+        chunk = (path // group + turned) % parts
+
+        @pl.loop(0, group)
+        def _(step):
+            source = chunk * group + (path + step) % group
+
+            @pl.when(jnp.logical_or(source != path, jnp.logical_not(is_home)))
+            def _():
+                field_arrival(source).wait_recv()
+
+            @pl.when(jnp.logical_and(source == path, is_home))
+            def _():
+                home_copy.wait()
+
+            for turn in range(1, row_count):
+                pass_copy(source, turn).start()
+
+        @pl.loop(0, group)
+        def _(step):
+            for turn in range(1, row_count):
+                pass_arrival(chunk * group + step, turn).wait_recv()
+
         def rows_of(part):
             return jnp.concatenate(
                 [
@@ -302,7 +306,7 @@
     def _(turn):
         chunk = (path // group + 1 + turn) % parts
         rows = pl.ds(pl.multiple_of(chunk * tall, tall), tall)
-        intensity = slab_second(both, middle, rows, gain * gain * (CASES / ghosts))
+        intensity = slab_second(both, middle, rows, gain * gain)
         bright[pl.ds(chunk * group, group)] = intensity.reshape(group, piece, slab_cells)
 
         @pl.loop(0, group)
@@ -414,7 +418,8 @@
     pair, case = small[-2:]
     ghosts = case.shape[0]
     if piece % 16 == 0 and ghosts == paths and paths % (2 * row_count) == 0 and row_count > 1:
-        return whole(cells, paths, row_count, main_field, table, *small)
+        total = whole(cells, paths, row_count, main_field, table, *small)
+        return total * (CASES / ghosts)
     per_device = ghosts // paths
     picked = main_field[:, case * SURF + pair[0]]
     picked = picked.reshape(2, paths, per_device, piece, slab_cells)

time: 40.5 us -> 35.6 us (0.88)
  the two profiles are of different devices: /device:TPU:0 before, /device:TPU:19 now
where the time goes in v3:
time: 35.6 us; the launch traced here: 35.4 us
  Pallas kernels  33.9 us (95%)
  other arithmetic  1.57 us (4%)
    pallas_call x1, Pallas kernels, whole(): pl.pallas_call(functools.partial(whole_kernel, cells, paths, row_count),...  33.9 us
    mul x1, other arithmetic, local(): return total * (CASES / ghosts)  1.57 us

profile of v3, /device:TPU:19, one launch (start us, length us, event | category | flops | bytes accessed | tf_op | source)
XLA Modules:
  0.0 35.4 jit_solution(6294904924535670969)
XLA Ops:
  0.0 33.9 %shard_map.82 = f32[4,32,256]{2,1,0:T(8,128)} custom-call(bf16[2,36,32,256]{3,2,1,0:T(8,128)(2,1)} %field_hbm.1, bf16[2,512,512]{2,1,0:T(8,128)(2,1)} %constant.4.clone.table_hbm, f32[9]{0:T(128)} %rest_0_.1, f32[9]{0:T(128)} %rest_1_.1, f32[9]{0:T(128)} %rest_2_.1, f32[4]{0:T(128)} %rest_3_.1, s32[2,16]{1,0:T(2,128)} %bitcast.1, s32[16]{0:T(128)} %rest_5_.1), custom_call_target="tpu_custom_call" | custom-call | tf_op jit(solution)/shard_map/pallas_call | solution.py:362
  33.9 1.6 %broadcast_multiply_fusion = f32[4,32,256]{2,1,0:T(8,128)} fusion(f32[4,32,256]{2,1,0:T(8,128)} %shard_map.82), kind=kLoop, calls=%fused_computation | loop fusion | flops 32768 | bytes 262144 | tf_op jit(solution)/shard_map/mul | solution.py:422
